TPU v7x, 256 devices: a whole 4x4x8 slice. The times are simulated.
256 devices in a mesh: row: 16 (over y_lo, z), col: 16 (over x, y_hi, core).
Axes of the slice: x: 4, y: 4 (y_hi: 2, y_lo: 2; y = y_hi * 2 + y_lo), z: 8, core: 2. Of those that a mesh axis runs over, the one named last changes fastest.
Arguments:
- object_field: float32 [2, 2, 4096, 4096], P(None, None, 'row', 'col'), may hold values from -4 to 4
- probe: float32 [2, 128, 128], replicated, may hold values from -6 to 6
- intensity: float32 [16, 128, 128, 128], P('row', 'col'), may hold values from 0 to 2
- offset_row: int32 [16, 128], P('row', 'col'), may hold values from 0 to 255
- offset_col: int32 [16, 128], P('row', 'col'), may hold values from 0 to 255
- live: int32 [16, 16], P('row', 'col'), may hold values from 1 to 8, as said below
Outputs:
- new_object: float32 [2, 2, 4096, 4096], P(None, None, 'row', 'col')
- new_probe: float32 [2, 128, 128], replicated
Inputs may be any that keep to these rules, and one draw needn't show every extreme that they name: Device (a, b) uses its first live[a, b] slots; at least one device uses all 8.
All inputs are finite; a program needn't handle non-finite values.
Results may differ from a plain program's by a relative error of at most 0.0003.
Values sent between devices are 32-bit elements; how exact they have to be, the bound alone decides.
No kernel may reach another device: no remote copies, remote signals or barrier semaphores. Data moves between devices by JAX's collectives and lax.ppermute only.
A program may use at most 64 MiB of HBM per device.

v0:
```python
import math
import jax
import jax.numpy as jnp
from jax import lax
from jax.sharding import PartitionSpec as P

STEP_OBJECT = 0.03
STEP_PROBE = 2.0
FRESNEL_PHASE = 60.0


def with_halo(block, sides, width):
    for axis, dim in sides:
        count = lax.axis_size(axis)
        forward = [(i, i + 1) for i in range(count - 1)]
        backward = [(target, source) for source, target in forward]
        low = lax.ppermute(
            lax.slice_in_dim(block, block.shape[dim] - width, None, axis=dim), axis, forward
        )
        high = lax.ppermute(lax.slice_in_dim(block, 0, width, axis=dim), axis, backward)
        block = jnp.concatenate([low, block, high], axis=dim)
    return block


def make_tables(width):
    index = jnp.arange(width, dtype=jnp.int32)
    product = index[:, None] * index[None, :] % width
    angle = 2.0 * math.pi / width * product.astype(jnp.float32)
    scale = 1.0 / math.sqrt(width)
    four_re = jnp.cos(angle) * scale
    four_im = -jnp.sin(angle) * scale
    freq = jnp.where(index < width // 2, index, index - width).astype(jnp.float32) / width
    phase = -FRESNEL_PHASE * (freq[:, None] ** 2 + freq[None, :] ** 2)
    return (four_re, four_im, jnp.cos(phase), jnp.sin(phase))


def transform(wave_re, wave_im, four_re, four_im):
    high = lax.Precision.HIGHEST
    right_re = jnp.einsum("kab,bc->kac", wave_re, four_re, precision=high) - jnp.einsum(
        "kab,bc->kac", wave_im, four_im, precision=high
    )
    right_im = jnp.einsum("kab,bc->kac", wave_re, four_im, precision=high) + jnp.einsum(
        "kab,bc->kac", wave_im, four_re, precision=high
    )
    out_re = jnp.einsum("ab,kbc->kac", four_re, right_re, precision=high) - jnp.einsum(
        "ab,kbc->kac", four_im, right_im, precision=high
    )
    out_im = jnp.einsum("ab,kbc->kac", four_im, right_re, precision=high) + jnp.einsum(
        "ab,kbc->kac", four_re, right_im, precision=high
    )
    return (out_re, out_im)


def window_grads(windows, probe, measured, active, tabs):
    four_re, four_im, prop_re, prop_im = tabs
    probe_re, probe_im = (probe[0], probe[1])
    first_re, first_im = (windows[:, 0, 0], windows[:, 0, 1])
    second_re, second_im = (windows[:, 1, 0], windows[:, 1, 1])
    wave_re = probe_re * first_re - probe_im * first_im
    wave_im = probe_re * first_im + probe_im * first_re
    spec_re, spec_im = transform(wave_re, wave_im, four_re, four_im)
    spec_re, spec_im = (
        spec_re * prop_re - spec_im * prop_im,
        spec_re * prop_im + spec_im * prop_re,
    )
    mid_re, mid_im = transform(spec_re, spec_im, four_re, -four_im)
    exit_re = mid_re * second_re - mid_im * second_im
    exit_im = mid_re * second_im + mid_im * second_re
    far_re, far_im = transform(exit_re, exit_im, four_re, four_im)
    weight = 2.0 * (far_re * far_re + far_im * far_im - measured) * active[:, None, None]
    chi_re, chi_im = transform(weight * far_re, weight * far_im, four_re, -four_im)
    back_re = second_re * chi_re + second_im * chi_im
    back_im = second_re * chi_im - second_im * chi_re
    grad2_re = mid_re * chi_re + mid_im * chi_im
    grad2_im = mid_re * chi_im - mid_im * chi_re
    spec_re, spec_im = transform(back_re, back_im, four_re, four_im)
    spec_re, spec_im = (
        spec_re * prop_re + spec_im * prop_im,
        spec_im * prop_re - spec_re * prop_im,
    )
    down_re, down_im = transform(spec_re, spec_im, four_re, -four_im)
    grad1_re = probe_re * down_re + probe_im * down_im
    grad1_im = probe_re * down_im - probe_im * down_re
    probe_gre = jnp.sum(first_re * down_re + first_im * down_im, axis=0)
    probe_gim = jnp.sum(first_re * down_im - first_im * down_re, axis=0)
    grads = jnp.stack([jnp.stack([grad1_re, grad1_im], 1), jnp.stack([grad2_re, grad2_im], 1)], 1)
    return (grads, jnp.stack([probe_gre, probe_gim]))


def squeeze_rim(grid, axis, half, tile):
    width = 2 * half
    return jnp.concatenate(
        [
            lax.slice_in_dim(grid, 0, half, axis=axis),
            lax.slice_in_dim(grid, width, tile, axis=axis),
            lax.slice_in_dim(grid, tile + half, tile + width, axis=axis),
        ],
        axis=axis,
    )


def on_device(object_field, probe, intensity, offset_row, offset_col, live):
    tile = object_field.shape[2]
    width = probe.shape[1]
    half = width // 2
    slot_count = offset_row.shape[1]
    extended = with_halo(object_field, (("row", 2), ("col", 3)), half)
    row_start = offset_row[0]
    col_start = offset_col[0]
    active = (jnp.arange(slot_count, dtype=jnp.int32) < live[0, 0]).astype(jnp.float32)
    windows = jax.vmap(
        lambda rstart, cstart: lax.dynamic_slice(
            extended, (jnp.int32(0), jnp.int32(0), rstart, cstart), (2, 2, width, width)
        )
    )(row_start, col_start)
    grads, probe_part = window_grads(windows, probe, intensity[0], active, make_tables(width))

    def add_slot(slot, accum_grad):
        start = (jnp.int32(0), jnp.int32(0), row_start[slot], col_start[slot])
        current = lax.dynamic_slice(accum_grad, start, (2, 2, width, width))
        return lax.dynamic_update_slice(accum_grad, current + grads[slot], start)

    grad_ext = lax.fori_loop(0, slot_count, add_slot, jnp.zeros(extended.shape, jnp.float32))
    row_set = squeeze_rim(grad_ext[:, :, :, half : tile + half], 2, half, tile)
    col_set = squeeze_rim(grad_ext[:, :, half : tile + half, :], 3, half, tile)
    corner_set = squeeze_rim(squeeze_rim(grad_ext, 2, half, tile), 3, half, tile)
    packed = jnp.concatenate([row_set, col_set, corner_set], axis=0)
    returned = with_halo(packed, (("row", 2), ("col", 3)), half)
    from_rows = returned[0:2]
    from_cols = returned[2:4]
    from_corner = returned[4:6]
    inner = grad_ext[:, :, half : tile + half, half : tile + half]
    inner = inner.at[:, :, :half, :].add(from_rows[:, :, :half, half : tile + half])
    inner = inner.at[:, :, tile - half :, :].add(from_rows[:, :, tile + half :, half : tile + half])
    inner = inner.at[:, :, :, :half].add(from_cols[:, :, half : tile + half, :half])
    inner = inner.at[:, :, :, tile - half :].add(from_cols[:, :, half : tile + half, tile + half :])
    inner = inner.at[:, :, :half, :half].add(from_corner[:, :, :half, :half])
    inner = inner.at[:, :, :half, tile - half :].add(from_corner[:, :, :half, tile + half :])
    inner = inner.at[:, :, tile - half :, :half].add(from_corner[:, :, tile + half :, :half])
    inner = inner.at[:, :, tile - half :, tile - half :].add(
        from_corner[:, :, tile + half :, tile + half :]
    )
    probe_total = lax.psum(probe_part, ("row", "col"))
    count_all = slot_count * lax.axis_size("row") * lax.axis_size("col")
    new_object = object_field - STEP_OBJECT * inner
    new_probe = probe - STEP_PROBE / count_all * probe_total
    return (new_object, new_probe)


def solution(mesh):
    placed = (
        P(None, None, "row", "col"),
        P(),
        P("row", "col", None, None),
        P("row", "col"),
        P("row", "col"),
        P("row", "col"),
    )
    return jax.shard_map(
        on_device,
        mesh=mesh,
        in_specs=placed,
        out_specs=(P(None, None, "row", "col"), P()),
        check_vma=False,
    )
```

profile of v0, /device:TPU:8, one launch (start us, length us, event | category | flops | bytes accessed | tf_op | source)
XLA Modules:
  0.0 537.3 jit_solution(3753956804749507980)
XLA Ops:
  7.2 1.6 copy.140
  9.0 7.6 %collective-permute-start.1 = (f32[2,2,64,256]{2,3,1,0:T(8,128)S(1)}, f32[2,2,64,256]{2,3,1,0:T(8,128)S(1)}, u32[]{:S(2)}, u32[]{:S(2)}) collective-permute-start(f32[2,2,64,256]{2,3,1,0:T(8,128)S(1)} %get-tuple-element.283), channel_id=1, source_target_pairs={{16,0},{32,16},{48,32},{64,48},{80,64},{96,80},{112,96},{128,112},... | collective-permute-start | bytes 786440 | tf_op jit(solution)/shard_map/ppermute | solution.py:20
  16.7 1.9 collective-permute-start
  18.8 9.1 %collective-permute-done.1 = f32[2,2,64,256]{2,3,1,0:T(8,128)S(1)} collective-permute-done((f32[2,2,64,256]{2,3,1,0:T(8,128)S(1)}, f32[2,2,64,256]{2,3,1,0:T(8,128)S(1)}, u32[]{:S(2)}, u32[]{:S(2)}) %collective-permute-start.1) | collective-permute-done | bytes 262176 | tf_op jit(solution)/shard_map/ppermute | solution.py:20
  27.9 6.5 %collective-permute-done = f32[2,2,64,256]{2,3,1,0:T(8,128)S(1)} collective-permute-done((f32[2,2,64,256]{2,3,1,0:T(8,128)S(1)}, f32[2,2,64,256]{2,3,1,0:T(8,128)S(1)}, u32[]{:S(2)}, u32[]{:S(2)}) %collective-permute-start) | collective-permute-done | bytes 262176 | tf_op jit(solution)/shard_map/ppermute | solution.py:17
  34.3 1.2 pad_maximum_fusion.12
  35.6 1.3 collective-permute-start.3
  36.9 3.8 collective-permute-start.2
  40.7 2.0 copy.173
  43.9 3.5 pad_maximum_fusion.1
  47.4 27.8 %while.23 = (s32[]{:T(128)}, f32[2,2,384,384]{2,3,1,0:T(8,128)}, s32[8,4]{0,1:T(4,128)S(1)}, f32[8,2,2,128,128]{3,4,0,2,1:T(8,128)S(1)}, s32[]{:T(128)}) while((s32[]{:T(128)}, f32[2,2,384,384]{2,3,1,0:T(8,128)}, s32[8,4]{0,1:T(4,128)S(1)}, f32[8,2,2,128,128]{3,4,0,2,1:T(8,128)S(1)}, s32[]{:T(128)}) %tuple.110), condition=%wide.while_cond.8, body=%wide.while_body.8.sunk | while | flops 2 | bytes 2097285 | solution.py:112
  48.0 2.4 constant_dynamic-slice_fusion.8
  51.4 2.4 constant_dynamic-slice_fusion.8
  54.8 2.4 constant_dynamic-slice_fusion.8
  58.3 2.4 constant_dynamic-slice_fusion.8
  61.7 2.4 constant_dynamic-slice_fusion.8
  65.1 2.4 constant_dynamic-slice_fusion.8
  68.5 2.4 constant_dynamic-slice_fusion.8
  71.9 2.4 constant_dynamic-slice_fusion.8
  75.1 1.2 fusion.102
  76.3 1.2 fusion.67
  77.6 1.2 convolution_subtract_fusion.11
  81.0 1.2 convolution_add_fusion.11
  84.5 1.2 fusion.30
  85.7 1.4 fusion.29
  87.1 1.2 convolution_subtract_fusion.9
  90.6 1.2 convolution_add_fusion.9
  98.6 1.3 fusion.58
  110.2 1.5 fusion.4
  111.7 1.2 fusion.18
  122.1 1.4 fusion.32
  123.5 1.2 fusion.31
  124.7 1.2 convolution_subtract_fusion.1
  128.2 1.2 convolution_add_fusion.1
  130.6 1.2 fusion.22
  131.9 1.5 pad_maximum_fusion.2
  133.5 77.9 %while.22 = (s32[]{:T(128)}, f32[2,2,384,384]{3,2,1,0:T(8,128)S(1)}, s32[8]{0:T(128)S(1)}, s32[8]{0:T(128)S(1)}, f32[8,2,2,128,128]{3,4,0,2,1:T(8,128)}, /*index=5*/s32[]{:T(128)}, s32[]{:T(128)}, s32[]{:T(128)}) while((s32[]{:T(128)}, f32[2,2,384,384]{3,2,1,0:T(8,128)S(1)}, s32[8]{0:T(128)S(1)}, s32[8]{0:T(128)S(1)}, ...), condition=%wide.region_1.2_spmd, body=%wide.region_0.1_spmd.sunk | while | flops 65544 | bytes 2359497 | solution.py:123
  139.9 3.2 dynamic_update_slice.8
  149.4 3.1 dynamic_update_slice.8
  158.9 3.4 dynamic_update_slice.8
  168.7 3.4 dynamic_update_slice.8
  178.4 3.4 dynamic_update_slice.8
  188.2 3.4 dynamic_update_slice.8
  198.0 3.4 dynamic_update_slice.8
  207.8 3.4 dynamic_update_slice.8
  213.0 1.9 collective-permute-start.4
  214.9 6.0 %collective-permute-start.5 = (f32[6,2,64,256]{3,2,1,0:T(8,128)S(1)}, f32[6,2,64,256]{3,2,1,0:T(8,128)S(1)}, u32[]{:S(2)}, u32[]{:S(2)}) collective-permute-start(f32[6,2,64,256]{3,2,1,0:T(8,128)S(1)} %get-tuple-element.252), channel_id=1, source_target_pairs={{16,0},{32,16},{48,32},{64,48},{80,64},{96,80},{112,96},{128,112},... | collective-permute-start | bytes 2359304 | tf_op jit(solution)/shard_map/ppermute | solution.py:20
  221.0 12.3 %collective-permute-done.4 = f32[6,2,64,256]{3,2,1,0:T(8,128)S(1)} collective-permute-done((f32[6,2,64,256]{3,2,1,0:T(8,128)S(1)}, f32[6,2,64,256]{3,2,1,0:T(8,128)S(1)}, u32[]{:S(2)}, u32[]{:S(2)}) %collective-permute-start.4) | collective-permute-done | bytes 786464 | tf_op jit(solution)/shard_map/ppermute | solution.py:17
  233.3 1.7 collective-permute-done.5
  235.1 2.3 pad_maximum_fusion
  237.3 2.9 fusion.370
  240.3 2.8 copy.199
  243.1 6.9 %collective-permute-start.6 = (f32[6,2,384,64]{2,3,1,0:T(8,128)}, f32[6,2,384,64]{2,3,1,0:T(8,128)}, u32[]{:S(2)}, u32[]{:S(2)}) collective-permute-start(f32[6,2,384,64]{2,3,1,0:T(8,128)} %copy.199), channel_id=1, source_target_pairs={{0,1},{1,2},{2,3},{3,4},{4,5},{5,6},{6,7},{7,8},{8,9},{9,10},{10,1... | collective-permute-start | bytes 3538952 | tf_op jit(solution)/shard_map/ppermute | solution.py:17
  250.8 2.8 copy.201
  253.6 1.3 collective-permute-start.7
  256.6 247.3 %all-reduce.2.cloned.1.call-done = f32[2,128,128]{1,2,0:T(8,128)} async-done(((f32[2,128,128]{1,2,0:T(8,128)}), f32[2,128,128]{1,2,0:T(8,128)}) %all-reduce.2.cloned.1.call-update) | async-done | bytes 131088 | tf_op jit(solution)/shard_map/psum | solution.py:143
  503.8 1.6 multiply_subtract_fusion.3
  505.4 1.7 copy.208
  510.6 2.3 scatter-add.30
  515.6 2.4 scatter-add.31
  518.0 1.2 scatter-add.34
  520.4 1.9 add_select_fusion
  522.3 3.5 scatter-add.35
  527.0 2.0 scatter-add.39
  (190 shorter events, 77.8 us)
Async XLA Ops:
  7.2 11.5 %copy-start.8 = (s32[1,8]{1,0:T(1,128)S(1)}, s32[1,8]{1,0:T(1,128)}, u32[]{:S(2)}) copy-start(s32[1,8]{1,0:T(1,128)} %param.27) | copy-start | bytes 100
  7.2 11.5 %copy-start.9 = (s32[1,8]{1,0:T(1,128)S(1)}, s32[1,8]{1,0:T(1,128)}, u32[]{:S(2)}) copy-start(s32[1,8]{1,0:T(1,128)} %param.28) | copy-start | bytes 100
  7.2 11.6 %copy-start.6 = (f32[2,128,128]{2,1,0:T(8,128)S(1)}, f32[2,128,128]{2,1,0:T(8,128)}, u32[]{:S(2)}) copy-start(f32[2,128,128]{2,1,0:T(8,128)} %param.25) | copy-start | bytes 393220
  7.2 496.6 %all-reduce.2.cloned.1.call-start = ((), (), s32[]{:S(2)}) async-start(), calls=%async_computation | async-start | bytes 262144 | tf_op jit(solution)/shard_map/psum | solution.py:143
  9.0 18.8 %collective-permute-start.1 = (f32[2,2,64,256]{2,3,1,0:T(8,128)S(1)}, f32[2,2,64,256]{2,3,1,0:T(8,128)S(1)}, u32[]{:S(2)}, u32[]{:S(2)}) collective-permute-start(f32[2,2,64,256]{2,3,1,0:T(8,128)S(1)} %get-tuple-element.283), channel_id=1, source_target_pairs={{16,0},{32,16},{48,32},{64,48},{80,64},{96,80},{112,96},{128,112},... | collective-permute-start | bytes 786440 | tf_op jit(solution)/shard_map/ppermute | solution.py:20
  16.7 17.6 %collective-permute-start = (f32[2,2,64,256]{2,3,1,0:T(8,128)S(1)}, f32[2,2,64,256]{2,3,1,0:T(8,128)S(1)}, u32[]{:S(2)}, u32[]{:S(2)}) collective-permute-start(f32[2,2,64,256]{2,3,1,0:T(8,128)S(1)} %get-tuple-element.282), channel_id=1, source_target_pairs={{0,16},{16,32},{32,48},{48,64},{64,80},{80,96},{96,112},{112,128},... | collective-permute-start | bytes 786440 | tf_op jit(solution)/shard_map/ppermute | solution.py:17
  27.9 6.5 %copy-start.1 = (f32[2,2,64,256]{2,3,1,0:T(8,128)}, f32[2,2,64,256]{2,3,1,0:T(8,128)S(1)}, u32[]{:S(2)}) copy-start(f32[2,2,64,256]{2,3,1,0:T(8,128)S(1)} %collective-permute-done.1) | copy-start | bytes 786436
  34.3 1.2 copy-start.2
  35.6 8.3 %collective-permute-start.3 = (f32[2,2,384,64]{2,3,1,0:T(8,128)}, f32[2,2,384,64]{2,3,1,0:T(8,128)}, u32[]{:S(2)}, u32[]{:S(2)}) collective-permute-start(f32[2,2,384,64]{2,3,1,0:T(8,128)} %get-tuple-element.267), channel_id=1, source_target_pairs={{1,0},{2,1},{3,2},{4,3},{5,4},{6,5},{7,6},{8,7},{9,8},{10,9},{11,1... | collective-permute-start | bytes 1179656 | tf_op jit(solution)/shard_map/ppermute | solution.py:20
  36.9 7.0 %collective-permute-start.2 = (f32[2,2,384,64]{2,3,1,0:T(8,128)}, f32[2,2,384,64]{2,3,1,0:T(8,128)}, u32[]{:S(2)}, u32[]{:S(2)}) collective-permute-start(f32[2,2,384,64]{2,3,1,0:T(8,128)} %get-tuple-element.266), channel_id=1, source_target_pairs={{0,1},{1,2},{2,3},{3,4},{4,5},{5,6},{6,7},{7,8},{8,9},{9,10},{10,1... | collective-permute-start | bytes 1179656 | tf_op jit(solution)/shard_map/ppermute | solution.py:17
  97.5 4.8 copy-start.3
  213.0 20.3 %collective-permute-start.4 = (f32[6,2,64,256]{3,2,1,0:T(8,128)S(1)}, f32[6,2,64,256]{3,2,1,0:T(8,128)S(1)}, u32[]{:S(2)}, u32[]{:S(2)}) collective-permute-start(f32[6,2,64,256]{3,2,1,0:T(8,128)S(1)} %get-tuple-element.253), channel_id=1, source_target_pairs={{0,16},{16,32},{32,48},{48,64},{64,80},{80,96},{96,112},{112,128},... | collective-permute-start | bytes 2359304 | tf_op jit(solution)/shard_map/ppermute | solution.py:17
  214.9 20.1 %collective-permute-start.5 = (f32[6,2,64,256]{3,2,1,0:T(8,128)S(1)}, f32[6,2,64,256]{3,2,1,0:T(8,128)S(1)}, u32[]{:S(2)}, u32[]{:S(2)}) collective-permute-start(f32[6,2,64,256]{3,2,1,0:T(8,128)S(1)} %get-tuple-element.252), channel_id=1, source_target_pairs={{16,0},{32,16},{48,32},{64,48},{80,64},{96,80},{112,96},{128,112},... | collective-permute-start | bytes 2359304 | tf_op jit(solution)/shard_map/ppermute | solution.py:20
  233.3 4.0 copy-start.4
  235.1 2.3 copy-start.5
  240.3 9.7 %copy-start.7 = (f32[2,128,128]{2,1,0:T(8,128)S(1)}, f32[2,128,128]{2,1,0:T(8,128)}, u32[]{:S(2)}) copy-start(f32[2,128,128]{2,1,0:T(8,128)} %param.25) | copy-start | bytes 393220
  240.3 9.8 %copy-start.10 = (s32[4]{0:T(128)S(1)}, s32[4]{0:T(128)}, u32[]{:S(2)}) copy-start(s32[4]{0:T(128)} %constant.288.clone.1) | copy-start | bytes 52
  243.1 266.0 %collective-permute-start.6 = (f32[6,2,384,64]{2,3,1,0:T(8,128)}, f32[6,2,384,64]{2,3,1,0:T(8,128)}, u32[]{:S(2)}, u32[]{:S(2)}) collective-permute-start(f32[6,2,384,64]{2,3,1,0:T(8,128)} %copy.199), channel_id=1, source_target_pairs={{0,1},{1,2},{2,3},{3,4},{4,5},{5,6},{6,7},{7,8},{8,9},{9,10},{10,1... | collective-permute-start | bytes 3538952 | tf_op jit(solution)/shard_map/ppermute | solution.py:17
  253.6 259.2 %collective-permute-start.7 = (f32[6,2,384,64]{2,3,1,0:T(8,128)}, f32[6,2,384,64]{2,3,1,0:T(8,128)}, u32[]{:S(2)}, u32[]{:S(2)}) collective-permute-start(f32[6,2,384,64]{2,3,1,0:T(8,128)} %copy.201), channel_id=1, source_target_pairs={{1,0},{2,1},{3,2},{4,3},{5,4},{6,5},{7,6},{8,7},{9,8},{10,9},{11,1... | collective-permute-start | bytes 3538952 | tf_op jit(solution)/shard_map/ppermute | solution.py:20
  515.6 13.5 %copy-start = (f32[2,2,256,256]{3,2,1,0:T(8,128)S(1)}, f32[2,2,256,256]{3,2,1,0:T(8,128)}, u32[]{:S(2)}) copy-start(f32[2,2,256,256]{3,2,1,0:T(8,128)} %param.24) | copy-start | bytes 3145732
Sparse Core Ops, SparseCore 0:
  255.7 248.0 all-reduce.1
where the time goes:
time: 542 us; the launch traced here: 537 us
  waiting for transfers between devices  277 us (51%)
  local copies, waits for them, and re-layouts  106 us (20%)
  matrix products  56.2 us (10%)
  loops' own time  32.5 us (6%)
  starting transfers between devices  30.8 us (6%)
  other arithmetic  19.2 us (4%)
  between operations  15.8 us (3%)
    psum x1, waiting for transfers between devices, on_device(): probe_total = lax.psum(probe_part, ('row', 'col'))  247 us
    another operation x1, loops' own time, on_device(): lax.fori_loop(0, slot_count, add_slot, jnp.zeros(extended.shape, jnp.floa...  31.7 us
    gather x48, local copies, waits for them, and re-layouts  27 us
    dynamic_update_slice x8, local copies, waits for them, and re-layouts, add_slot(): return lax.dynamic_update_slice(accum_grad, current + grads[slot], start)  26.8 us
    ppermute x4, waiting for transfers between devices, with_halo(): lax.ppermute(lax.slice_in_dim(block, block.shape[dim] - width, None, axis...  18.8 us
    ppermute x4, starting transfers between devices, with_halo(): lax.ppermute(lax.slice_in_dim(block, 0, width, axis=dim), axis, backward)  16.2 us
    ppermute x4, starting transfers between devices, with_halo(): lax.ppermute(lax.slice_in_dim(block, block.shape[dim] - width, None, axis...  14.5 us
  transfers between devices with their start and end apart: 9, of which 5 were waited for; matrix products, arithmetic and copies ran while one was open for 3% of the time, Pallas kernels for 0%

commit v1 on v0

--- a/solution.py
+++ b/solution.py
@@ -140,7 +140,7 @@
     inner = inner.at[:, :, tile - half :, tile - half :].add(
         from_corner[:, :, tile + half :, tile + half :]
     )
-    probe_total = lax.psum(probe_part, ("row", "col"))
+    probe_total = jnp.sum(lax.all_gather(probe_part, ("row", "col")), axis=0)
     count_all = slot_count * lax.axis_size("row") * lax.axis_size("col")
     new_object = object_field - STEP_OBJECT * inner
     new_probe = probe - STEP_PROBE / count_all * probe_total

time: 542 us -> 651 us (1.20)
  waiting for transfers between devices: 277 us -> 371 us
  other arithmetic: 19.2 us -> 31.5 us
    all_gather x0 -> x1, waiting for transfers between devices: none -> 333 us  [on_device(): probe_total = jnp.sum(lax.all_gather(probe_part, ('row', 'col')), axis=0)]
    psum x1 -> x0, waiting for transfers between devices: 247 us -> none  [on_device(): probe_total = lax.psum(probe_part, ('row', 'col'))]
    reduce_sum x0 -> x1, other arithmetic: none -> 12.2 us  [on_device(): probe_total = jnp.sum(lax.all_gather(probe_part, ('row', 'col')), axis=0)]
  transfers between devices with their start and end apart: 9 -> 9, of which waited for: 5 -> 5; matrix products, arithmetic and copies ran while one was open for 3% -> 14% of each run, Pallas kernels for 0% -> 0%
where the time goes in v1:
time: 651 us; the launch traced here: 642 us
  waiting for transfers between devices  371 us (57%)
  local copies, waits for them, and re-layouts  105 us (16%)
  matrix products  58.2 us (9%)
  loops' own time  32.5 us (5%)
  other arithmetic  31.5 us (5%)
  starting transfers between devices  28.3 us (4%)
  between operations  15.8 us (2%)
    all_gather x1, waiting for transfers between devices, on_device(): probe_total = jnp.sum(lax.all_gather(probe_part, ('row', 'col')), axis=0)  333 us
    another operation x1, loops' own time, on_device(): lax.fori_loop(0, slot_count, add_slot, jnp.zeros(extended.shape, jnp.floa...  31.7 us
    dynamic_update_slice x8, local copies, waits for them, and re-layouts, add_slot(): return lax.dynamic_update_slice(accum_grad, current + grads[slot], start)  26.8 us
    gather x48, local copies, waits for them, and re-layouts  26.4 us
    ppermute x4, waiting for transfers between devices, with_halo(): lax.ppermute(lax.slice_in_dim(block, block.shape[dim] - width, None, axis...  23.8 us
    ppermute x4, starting transfers between devices, with_halo(): lax.ppermute(lax.slice_in_dim(block, 0, width, axis=dim), axis, backward)  16.2 us
    ppermute x4, waiting for transfers between devices, with_halo(): lax.ppermute(lax.slice_in_dim(block, 0, width, axis=dim), axis, backward)  13.9 us
  transfers between devices with their start and end apart: 9, of which 5 were waited for; matrix products, arithmetic and copies ran while one was open for 14% of the time, Pallas kernels for 0%

profile of v1, /device:TPU:8, one launch (start us, length us, event | category | flops | bytes accessed | tf_op | source)
XLA Modules:
  0.0 641.8 jit_solution(11726159215069737888)
XLA Ops:
  7.2 1.6 copy.139
  9.0 7.6 %collective-permute-start.1 = (f32[2,2,64,256]{2,3,1,0:T(8,128)S(1)}, f32[2,2,64,256]{2,3,1,0:T(8,128)S(1)}, u32[]{:S(2)}, u32[]{:S(2)}) collective-permute-start(f32[2,2,64,256]{2,3,1,0:T(8,128)S(1)} %get-tuple-element.281), channel_id=1, source_target_pairs={{16,0},{32,16},{48,32},{64,48},{80,64},{96,80},{112,96},{128,112},... | collective-permute-start | bytes 786440 | tf_op jit(solution)/shard_map/ppermute | solution.py:20
  16.7 1.9 collective-permute-start
  18.8 9.1 %collective-permute-done.1 = f32[2,2,64,256]{2,3,1,0:T(8,128)S(1)} collective-permute-done((f32[2,2,64,256]{2,3,1,0:T(8,128)S(1)}, f32[2,2,64,256]{2,3,1,0:T(8,128)S(1)}, u32[]{:S(2)}, u32[]{:S(2)}) %collective-permute-start.1) | collective-permute-done | bytes 262176 | tf_op jit(solution)/shard_map/ppermute | solution.py:20
  27.9 6.5 %collective-permute-done = f32[2,2,64,256]{2,3,1,0:T(8,128)S(1)} collective-permute-done((f32[2,2,64,256]{2,3,1,0:T(8,128)S(1)}, f32[2,2,64,256]{2,3,1,0:T(8,128)S(1)}, u32[]{:S(2)}, u32[]{:S(2)}) %collective-permute-start) | collective-permute-done | bytes 262176 | tf_op jit(solution)/shard_map/ppermute | solution.py:17
  34.3 1.2 pad_maximum_fusion.12
  35.6 1.3 collective-permute-start.3
  36.9 3.8 collective-permute-start.2
  40.7 2.0 copy.172
  44.4 3.5 pad_maximum_fusion.1
  47.9 27.2 %while.23 = (s32[]{:T(128)}, f32[2,2,384,384]{2,3,1,0:T(8,128)}, s32[8,4]{0,1:T(4,128)S(1)}, f32[8,2,2,128,128]{3,4,0,2,1:T(8,128)S(1)}, s32[]{:T(128)}) while((s32[]{:T(128)}, f32[2,2,384,384]{2,3,1,0:T(8,128)}, s32[8,4]{0,1:T(4,128)S(1)}, f32[8,2,2,128,128]{3,4,0,2,1:T(8,128)S(1)}, s32[]{:T(128)}) %tuple.109), condition=%wide.while_cond.8, body=%wide.while_body.8.sunk | while | flops 2 | bytes 2097285 | solution.py:112
  48.5 2.4 constant_dynamic-slice_fusion.8
  51.8 2.4 constant_dynamic-slice_fusion.8
  55.2 2.4 constant_dynamic-slice_fusion.8
  58.5 2.4 constant_dynamic-slice_fusion.8
  61.8 2.4 constant_dynamic-slice_fusion.8
  65.2 2.4 constant_dynamic-slice_fusion.8
  68.5 2.4 constant_dynamic-slice_fusion.8
  71.9 2.4 constant_dynamic-slice_fusion.8
  75.1 1.2 fusion.102
  76.3 1.2 fusion.67
  77.5 1.2 convolution_subtract_fusion.11
  80.9 1.2 convolution_add_fusion.11
  84.4 1.2 fusion.30
  85.6 1.4 fusion.29
  87.0 1.2 convolution_subtract_fusion.9
  90.5 1.2 convolution_add_fusion.9
  98.5 1.3 fusion.58
  102.1 1.2 fusion.25
  110.1 1.5 fusion.4
  111.7 2.2 fusion.18
  123.0 1.4 fusion.32
  124.4 1.2 fusion.31
  125.6 1.2 convolution_subtract_fusion.1
  129.1 1.2 convolution_add_fusion.1
  131.4 2.2 fusion.22
  135.7 1.4 pad_maximum_fusion.2
  137.3 77.9 %while.22 = (s32[]{:T(128)}, f32[2,2,384,384]{3,2,1,0:T(8,128)S(1)}, s32[8]{0:T(128)S(1)}, s32[8]{0:T(128)S(1)}, f32[8,2,2,128,128]{3,4,0,2,1:T(8,128)}, /*index=5*/s32[]{:T(128)}, s32[]{:T(128)}, s32[]{:T(128)}) while((s32[]{:T(128)}, f32[2,2,384,384]{3,2,1,0:T(8,128)S(1)}, s32[8]{0:T(128)S(1)}, s32[8]{0:T(128)S(1)}, ...), condition=%wide.region_1.2_spmd, body=%wide.region_0.1_spmd.sunk | while | flops 65544 | bytes 2359497 | solution.py:123
  143.6 3.2 dynamic_update_slice.8
  153.2 3.1 dynamic_update_slice.8
  162.6 3.4 dynamic_update_slice.8
  172.4 3.4 dynamic_update_slice.8
  182.2 3.4 dynamic_update_slice.8
  192.0 3.4 dynamic_update_slice.8
  201.7 3.4 dynamic_update_slice.8
  211.5 3.4 dynamic_update_slice.8
  216.8 1.9 collective-permute-start.4
  218.7 6.0 collective-permute-start.5
  224.7 17.4 %collective-permute-done.4 = f32[6,2,64,256]{3,2,1,0:T(8,128)S(1)} collective-permute-done((f32[6,2,64,256]{3,2,1,0:T(8,128)S(1)}, f32[6,2,64,256]{3,2,1,0:T(8,128)S(1)}, u32[]{:S(2)}, u32[]{:S(2)}) %collective-permute-start.4) | collective-permute-done | bytes 786464 | tf_op jit(solution)/shard_map/ppermute | solution.py:17
  242.1 4.8 collective-permute-done.5
  246.9 2.3 pad_maximum_fusion
  249.2 3.0 fusion.370
  252.2 2.8 copy.198
  255.0 4.4 collective-permute-start.6
  259.4 2.8 copy.200
  262.2 1.3 collective-permute-start.7
  268.7 2.3 scatter-add.30
  273.8 2.4 scatter-add.31
  276.2 1.2 scatter-add.34
  278.6 2.0 add_select_fusion
  280.6 3.5 scatter-add.35
  285.3 2.0 scatter-add.39
  288.5 333.3 %all-gather.3.cloned.1.call-done = f32[512,128,128]{2,1,0:T(8,128)} async-done(((f32[2,128,128]{2,1,0:T(8,128)}), f32[512,128,128]{2,1,0:T(8,128)}) %all-gather.3.cloned.1.call-update) | async-done | bytes 33554448 | tf_op jit(solution)/shard_map/all_gather | solution.py:143
  621.8 12.2 %reduce_sum.29 = f32[2,128,128]{2,1,0:T(8,128)S(1)} reduce(f32[256,2,128,128]{3,2,1,0:T(8,128)} %bitcast.291, f32[]{:T(128)} %constant.275.clone.1), dimensions={0}, to_apply=%region_5.6 | reduce | flops 8355840 | bytes 33685508 | tf_op jit(solution)/shard_map/reduce_sum | solution.py:143
  (196 shorter events, 78.6 us)
Async XLA Ops:
  7.2 11.5 %copy-start.10 = (s32[1,8]{1,0:T(1,128)S(1)}, s32[1,8]{1,0:T(1,128)}, u32[]{:S(2)}) copy-start(s32[1,8]{1,0:T(1,128)} %param.27) | copy-start | bytes 100
  7.2 11.5 %copy-start.11 = (s32[1,8]{1,0:T(1,128)S(1)}, s32[1,8]{1,0:T(1,128)}, u32[]{:S(2)}) copy-start(s32[1,8]{1,0:T(1,128)} %param.28) | copy-start | bytes 100
  7.2 11.6 %copy-start.9 = (f32[2,128,128]{2,1,0:T(8,128)S(1)}, f32[2,128,128]{2,1,0:T(8,128)}, u32[]{:S(2)}) copy-start(f32[2,128,128]{2,1,0:T(8,128)} %param.25) | copy-start | bytes 393220
  7.2 614.6 %all-gather.3.cloned.1.call-start = ((), (), s32[]{:S(2)}) async-start(), calls=%async_computation | async-start | bytes 33685504 | tf_op jit(solution)/shard_map/all_gather | solution.py:143
  9.0 18.8 %collective-permute-start.1 = (f32[2,2,64,256]{2,3,1,0:T(8,128)S(1)}, f32[2,2,64,256]{2,3,1,0:T(8,128)S(1)}, u32[]{:S(2)}, u32[]{:S(2)}) collective-permute-start(f32[2,2,64,256]{2,3,1,0:T(8,128)S(1)} %get-tuple-element.281), channel_id=1, source_target_pairs={{16,0},{32,16},{48,32},{64,48},{80,64},{96,80},{112,96},{128,112},... | collective-permute-start | bytes 786440 | tf_op jit(solution)/shard_map/ppermute | solution.py:20
  16.7 17.6 %collective-permute-start = (f32[2,2,64,256]{2,3,1,0:T(8,128)S(1)}, f32[2,2,64,256]{2,3,1,0:T(8,128)S(1)}, u32[]{:S(2)}, u32[]{:S(2)}) collective-permute-start(f32[2,2,64,256]{2,3,1,0:T(8,128)S(1)} %get-tuple-element.280), channel_id=1, source_target_pairs={{0,16},{16,32},{32,48},{48,64},{64,80},{80,96},{96,112},{112,128},... | collective-permute-start | bytes 786440 | tf_op jit(solution)/shard_map/ppermute | solution.py:17
  27.9 6.5 %copy-start.1 = (f32[2,2,64,256]{2,3,1,0:T(8,128)}, f32[2,2,64,256]{2,3,1,0:T(8,128)S(1)}, u32[]{:S(2)}) copy-start(f32[2,2,64,256]{2,3,1,0:T(8,128)S(1)} %collective-permute-done.1) | copy-start | bytes 786436
  34.3 1.2 copy-start.3
  35.6 8.8 %collective-permute-start.3 = (f32[2,2,384,64]{2,3,1,0:T(8,128)}, f32[2,2,384,64]{2,3,1,0:T(8,128)}, u32[]{:S(2)}, u32[]{:S(2)}) collective-permute-start(f32[2,2,384,64]{2,3,1,0:T(8,128)} %get-tuple-element.265), channel_id=1, source_target_pairs={{1,0},{2,1},{3,2},{4,3},{5,4},{6,5},{7,6},{8,7},{9,8},{10,9},{11,1... | collective-permute-start | bytes 1179656 | tf_op jit(solution)/shard_map/ppermute | solution.py:20
  36.9 7.5 %collective-permute-start.2 = (f32[2,2,384,64]{2,3,1,0:T(8,128)}, f32[2,2,384,64]{2,3,1,0:T(8,128)}, u32[]{:S(2)}, u32[]{:S(2)}) collective-permute-start(f32[2,2,384,64]{2,3,1,0:T(8,128)} %get-tuple-element.264), channel_id=1, source_target_pairs={{0,1},{1,2},{2,3},{3,4},{4,5},{5,6},{6,7},{7,8},{8,9},{9,10},{10,1... | collective-permute-start | bytes 1179656 | tf_op jit(solution)/shard_map/ppermute | solution.py:17
  97.4 4.8 copy-start.4
  97.4 4.8 copy-start.13
  131.4 3.0 copy-start.2
  133.6 1.9 copy-start.5
  133.6 1.9 copy-start.6
  216.8 25.3 %collective-permute-start.4 = (f32[6,2,64,256]{3,2,1,0:T(8,128)S(1)}, f32[6,2,64,256]{3,2,1,0:T(8,128)S(1)}, u32[]{:S(2)}, u32[]{:S(2)}) collective-permute-start(f32[6,2,64,256]{3,2,1,0:T(8,128)S(1)} %get-tuple-element.251), channel_id=1, source_target_pairs={{0,16},{16,32},{32,48},{48,64},{64,80},{80,96},{96,112},{112,128},... | collective-permute-start | bytes 2359304 | tf_op jit(solution)/shard_map/ppermute | solution.py:17
  218.7 28.2 %collective-permute-start.5 = (f32[6,2,64,256]{3,2,1,0:T(8,128)S(1)}, f32[6,2,64,256]{3,2,1,0:T(8,128)S(1)}, u32[]{:S(2)}, u32[]{:S(2)}) collective-permute-start(f32[6,2,64,256]{3,2,1,0:T(8,128)S(1)} %get-tuple-element.250), channel_id=1, source_target_pairs={{16,0},{32,16},{48,32},{64,48},{80,64},{96,80},{112,96},{128,112},... | collective-permute-start | bytes 2359304 | tf_op jit(solution)/shard_map/ppermute | solution.py:20
  242.1 7.1 %copy-start.7 = (f32[6,2,64,256]{3,2,1,0:T(8,128)}, f32[6,2,64,256]{3,2,1,0:T(8,128)S(1)}, u32[]{:S(2)}) copy-start(f32[6,2,64,256]{3,2,1,0:T(8,128)S(1)} %collective-permute-done.4) | copy-start | bytes 2359300
  246.9 2.3 copy-start.8
  255.0 9.2 %copy-start.12 = (s32[4]{0:T(128)S(1)}, s32[4]{0:T(128)}, u32[]{:S(2)}) copy-start(s32[4]{0:T(128)} %constant.288.clone.1) | copy-start | bytes 52
  255.0 12.3 %collective-permute-start.6 = (f32[6,2,384,64]{2,3,1,0:T(8,128)}, f32[6,2,384,64]{2,3,1,0:T(8,128)}, u32[]{:S(2)}, u32[]{:S(2)}) collective-permute-start(f32[6,2,384,64]{2,3,1,0:T(8,128)} %copy.198), channel_id=1, source_target_pairs={{0,1},{1,2},{2,3},{3,4},{4,5},{5,6},{6,7},{7,8},{8,9},{9,10},{10,1... | collective-permute-start | bytes 3538952 | tf_op jit(solution)/shard_map/ppermute | solution.py:17
  262.2 8.8 %collective-permute-start.7 = (f32[6,2,384,64]{2,3,1,0:T(8,128)}, f32[6,2,384,64]{2,3,1,0:T(8,128)}, u32[]{:S(2)}, u32[]{:S(2)}) collective-permute-start(f32[6,2,384,64]{2,3,1,0:T(8,128)} %copy.200), channel_id=1, source_target_pairs={{1,0},{2,1},{3,2},{4,3},{5,4},{6,5},{7,6},{8,7},{9,8},{10,9},{11,1... | collective-permute-start | bytes 3538952 | tf_op jit(solution)/shard_map/ppermute | solution.py:20
  273.8 13.6 %copy-start = (f32[2,2,256,256]{3,2,1,0:T(8,128)S(1)}, f32[2,2,256,256]{3,2,1,0:T(8,128)}, u32[]{:S(2)}) copy-start(f32[2,2,256,256]{3,2,1,0:T(8,128)} %param.24) | copy-start | bytes 3145732
Sparse Core Ops, SparseCore 0:
  134.6 487.1 all-gather.2
